TPU v7x, 32 devices: a whole 2x2x4 slice. The times are simulated.
32 devices in a mesh: seq: 4 (over z), head: 2 (over y), dp: 4 (over x, core).
Axes of the slice: x: 2, y: 2, z: 4, core: 2. Of those that a mesh axis runs over, the one named last changes fastest.
Arguments:
- layer_input: bfloat16 [4, 512, 6144], P('dp', 'seq'), may hold values from -6 to 6
- queries: bfloat16 [4, 512, 1024], P('dp', 'seq', 'head'), may hold values from -6 to 6
- key_rows: bfloat16 [4, 512, 1024], P('dp', 'seq', 'head'), may hold values from -6 to 6
- value_rows: bfloat16 [4, 512, 1024], P('dp', 'seq', 'head'), may hold values from -6 to 6
- grad_out: bfloat16 [4, 512, 1024], P('dp', 'seq', 'head'), may hold values from -6 to 6
- log_decay: float32 [4, 512, 8], P('dp', 'seq', 'head'), may hold values from -2 to 0, as said below
Outputs:
- grad_query: bfloat16 [4, 512, 1024], P('dp', 'seq', 'head')
- grad_key: bfloat16 [4, 512, 1024], P('dp', 'seq', 'head')
- grad_value: bfloat16 [4, 512, 1024], P('dp', 'seq', 'head')
- key_weight_grad: bfloat16 [6144, 1024], P('seq', 'head')
- value_weight_grad: bfloat16 [6144, 1024], P('seq', 'head')
Inputs may be any that keep to these rules, and one draw needn't show every extreme that they name: log_decay is never positive.
All inputs are finite; a program needn't handle non-finite values.
Results may differ from a plain program's by a relative error of at most 0.0062.
Values may be sent and summed in bfloat16 or wider, within the bound.
A program may use at most 64 MiB of HBM per device.

v0:
```python
import math

import jax
import jax.numpy as jnp
from jax import lax
from jax.sharding import PartitionSpec as P

DH = 128


top_precision = lax.Precision.HIGHEST


def per_device(layer_input, queries, key_rows, value_rows, grad_out, log_decay):
    length = queries.shape[1]
    heads = log_decay.shape[2]
    query_three = queries[0].reshape(length, heads, DH)
    key_three = key_rows[0].reshape(length, heads, DH)
    triple_value = value_rows[0].reshape(length, heads, DH)
    triple_gradient = grad_out[0].reshape(length, heads, DH)
    running = jnp.cumsum(log_decay[0], axis=0)
    totals = running[-1]
    across = running.T
    positions = jnp.arange(length)
    lower_mask = positions[:, None] >= positions[None, :]
    decay_mask = jnp.where(
        lower_mask[None], jnp.exp(jnp.minimum(across[:, :, None] - across[:, None, :], 0.0)), 0.0
    )
    to_end = jnp.exp(totals[None, :] - running)
    from_start = jnp.exp(running)
    key_rows_scaled = (key_three * to_end[:, :, None]).astype(jnp.bfloat16)
    scaled_queries = (query_three * from_start[:, :, None]).astype(jnp.bfloat16)
    key_state = jnp.einsum(
        "nrx,nro->rxo", key_rows_scaled, triple_value, preferred_element_type=jnp.float32
    )
    query_state = jnp.einsum(
        "thq,thv->hqv", scaled_queries, triple_gradient, preferred_element_type=jnp.float32
    )
    every_key_row, all_queries, all_totals = (
        lax.all_gather(key_state[None], "seq", axis=0, tiled=True),
        lax.all_gather(query_state[None], "seq", axis=0, tiled=True),
        lax.all_gather(totals[None], "seq", axis=0, tiled=True),
    )
    count = lax.axis_size("seq")
    here = lax.axis_index("seq")
    through = jnp.cumsum(all_totals, axis=0)
    before = through - all_totals
    block_ids = jnp.arange(count)[:, None]
    own_before = lax.dynamic_index_in_dim(before, here, 0, keepdims=False)
    own_through = lax.dynamic_index_in_dim(through, here, 0, keepdims=False)
    leading_weight = jnp.where(
        block_ids < here, jnp.exp(jnp.minimum(own_before[None] - through, 0.0)), 0.0
    )
    late_weight = jnp.where(
        block_ids > here, jnp.exp(jnp.minimum(before - own_through[None], 0.0)), 0.0
    )
    prefix_running = jnp.einsum(
        "cp,cpqt->pqt", leading_weight, every_key_row, precision=top_precision
    )
    suffix = jnp.einsum("nh,nhqv->hqv", late_weight, all_queries, precision=top_precision)
    prefix_reduced = prefix_running.astype(jnp.bfloat16)
    suffix_low = suffix.astype(jnp.bfloat16)
    value_scores = jnp.einsum(
        "thv,jhv->htj", triple_gradient, triple_value, preferred_element_type=jnp.float32
    )
    value_weights = (value_scores * decay_mask).astype(jnp.bfloat16)
    key_scores = jnp.einsum(
        "thq,jhq->htj", query_three, key_three, preferred_element_type=jnp.float32
    )
    key_weights = (key_scores * decay_mask).astype(jnp.bfloat16)
    scale = 1.0 / DH
    query_grad = (
        jnp.einsum("htj,jhk->thk", value_weights, key_three, preferred_element_type=jnp.float32)
        + from_start[:, :, None]
        * jnp.einsum(
            "jfg,xjg->xjf", prefix_reduced, triple_gradient, preferred_element_type=jnp.float32
        )
    ) * scale
    key_grad = (
        jnp.einsum("htj,thq->jhq", value_weights, query_three, preferred_element_type=jnp.float32)
        + to_end[:, :, None]
        * jnp.einsum("hqv,jhv->jhq", suffix_low, triple_value, preferred_element_type=jnp.float32)
    ) * scale
    value_grad = (
        jnp.einsum("htj,thv->jhv", key_weights, triple_gradient, preferred_element_type=jnp.float32)
        + to_end[:, :, None]
        * jnp.einsum("hqv,jhq->jhv", suffix_low, key_three, preferred_element_type=jnp.float32)
    ) * scale
    grad_query = query_grad.astype(jnp.bfloat16).reshape(1, length, heads * DH)
    grad_key = key_grad.astype(jnp.bfloat16).reshape(1, length, heads * DH)
    grad_value = value_grad.astype(jnp.bfloat16).reshape(1, length, heads * DH)
    columns = lax.all_to_all(layer_input, "seq", split_axis=2, concat_axis=1, tiled=True)
    rows = columns[0]
    dims = (((0,), (0,)), ((), ()))
    key_part = lax.dot_general(
        rows,
        lax.all_gather(grad_key, "seq", axis=1, tiled=True)[0],
        dims,
        preferred_element_type=jnp.float32,
    )
    value_part = lax.dot_general(
        rows,
        lax.all_gather(grad_value, "seq", axis=1, tiled=True)[0],
        dims,
        preferred_element_type=jnp.float32,
    )
    factor = 1.0 / math.sqrt(lax.axis_size("dp") * lax.axis_size("seq") * layer_input.shape[1])
    key_summed, value_summed = lax.psum((key_part, value_part), "dp")
    key_weight_grad = (key_summed * factor).astype(jnp.bfloat16)
    value_weight_grad = (value_summed * factor).astype(jnp.bfloat16)
    return (grad_query, grad_key, grad_value, key_weight_grad, value_weight_grad)


def solution(mesh):
    return jax.shard_map(
        per_device,
        mesh=mesh,
        in_specs=(
            P("dp", "seq", None),
            P("dp", "seq", "head"),
            P("dp", "seq", "head"),
            P("dp", "seq", "head"),
            P("dp", "seq", "head"),
            P("dp", "seq", "head"),
        ),
        out_specs=(
            P("dp", "seq", "head"),
            P("dp", "seq", "head"),
            P("dp", "seq", "head"),
            P("seq", "head"),
            P("seq", "head"),
        ),
        check_vma=False,
    )
```

profile of v0, /device:TPU:0, one launch (start us, length us, event | category | flops | bytes accessed | tf_op | source)
XLA Modules:
  0.0 296.4 jit_solution(7479897676144758266)
XLA Ops:
  7.2 0.0 all-gather.8.cloned.1.call-start
  7.2 0.8 copy.80
  8.0 0.2 reduce_window_sum.22
  8.2 0.1 copy.84
  8.3 1.0 copy.88
  9.3 1.0 copy.119
  10.4 0.9 fusion.19
  11.3 6.8 %copy.96 = bf16[1,128,6144]{1,0,2:T(2,128)(2,1)S(1)} copy(bf16[1,128,6144]{2,1,0:T(8,128)(2,1)} %param.6) | data formatting | bytes 3145728 | tf_op args[0]
  18.2 0.5 broadcast.43
  18.7 34.4 %reduce.2 = bf16[6144,128]{1,0:T(8,128)(2,1)} reduce(bf16[6144,1,128]{2,1,0:T(2,128)(2,1)S(1)} %bitcast.97, bf16[]{:T(256)} %broadcast.43), dimensions={1}, to_apply=%bitcast.77.reduce_sub_computation | reduce | bytes 3145730
  53.1 3.7 %reshape.75 = bf16[4,2,98304]{2,1,0:T(2,128)(2,1)} reshape(bf16[6144,128]{1,0:T(8,128)(2,1)} %reduce.2) | data formatting | bytes 3145728
  56.8 6.5 %all-to-all-start = ((bf16[4,2,98304]{2,1,0:T(2,128)(2,1)}), bf16[4,2,98304]{2,1,0:T(2,128)(2,1)}, u32[]{:S(2)}, u32[]{:S(2)}) async-start(bf16[4,2,98304]{2,1,0:T(2,128)(2,1)} %reshape.75), calls=%async_computation | async-start | bytes 3145728 | tf_op jit(solution)/shard_map/all_to_all | solution.py:92
  63.3 0.1 copy.85
  63.3 0.1 reshape_squeeze.13
  63.4 0.1 copy.83
  63.5 0.9 fusion.18
  64.4 0.0 all-reduce.3.cloned.1.call-start
  64.5 44.7 %all-gather.2 = f32[4,1,4]{2,1,0:T(1,128)S(1)} all-gather(f32[1,1,4]{2,1,0:T(1,128)S(1)} %get-tuple-element.32), channel_id=1, replica_groups=mesh['seq'=4,'head'=2,'dp'=4] {'seq'}, dimensions={0}, use_global_device_ids=true | all-gather | bytes 80 | tf_op jit(solution)/shard_map/all_gather | solution.py:42
  109.1 0.1 copy.81
  109.3 0.1 select_bitcast_fusion
  109.4 0.2 fusion.12
  109.7 1.4 multiply_reduce_fusion
  111.1 0.1 copy.112
  111.2 0.2 fusion.5
  111.5 0.2 fusion.10
  111.6 23.9 %all_gather.18 = bf16[1,512,512]{1,2,0:T(8,128)(2,1)} all-gather(bf16[1,128,512]{1,2,0:T(8,128)(2,1)S(1)} %bitcast.104), channel_id=1, replica_groups=mesh['seq'=4,'head'=2,'dp'=4] {'seq'}, dimensions={1}, use_global_device_ids=true | all-gather | bytes 655360 | tf_op jit(solution)/shard_map/all_gather | solution.py:97
  135.5 0.2 fusion.4
  135.7 0.4 fusion.11
  136.1 14.7 %all_gather.19 = bf16[1,512,512]{1,2,0:T(8,128)(2,1)} all-gather(bf16[1,128,512]{1,2,0:T(8,128)(2,1)S(1)} %bitcast.117), channel_id=1, replica_groups=mesh['seq'=4,'head'=2,'dp'=4] {'seq'}, dimensions={1}, use_global_device_ids=true | all-gather | bytes 655360 | tf_op jit(solution)/shard_map/all_gather | solution.py:103
  150.8 3.1 %reshape.76 = bf16[6144,1,128]{2,1,0:T(2,128)(2,1)S(1)} reshape(bf16[4,2,98304]{2,1,0:T(2,128)(2,1)} %all-to-all-done) | data formatting | bytes 3145728
  153.8 1.3 copy.117
  155.2 1.8 copy.97
  157.0 2.6 convolution_bitcast_fusion
  159.6 2.6 convolution_bitcast_fusion.1
  162.3 0.1 select_bitcast_fusion.1
  162.4 0.1 copy.103
  162.5 0.7 copy-done.10
  163.2 0.2 convolution_bitcast_fusion.7
  163.4 0.8 copy.100
  164.1 0.8 copy.99
  164.9 3.6 %fusion.14 = f32[4,1,128,128]{3,1,2,0:T(1,128)S(1)} fusion(f32[4,4,1,1]{0,2,3,1:T(1,128)S(1)} %copy.103, f32[4,4,128,128]{3,2,1,0:T(8,128)} %bitcast.114), kind=kOutput, calls=%fused_computation.27 | convolution fusion | flops 3145728 | bytes 1310784 | tf_op jit(solution)/shard_map/cp,cpqt->pqt/dot_general | solution.py:57
  168.5 0.2 fusion.9
  168.7 0.8 copy.98
  169.5 112.8 %all-reduce.3.cloned.1.call-done = (f32[1536,512]{0,1:T(8,128)}, f32[1536,512]{0,1:T(8,128)}) async-done(((f32[1536,512]{0,1:T(8,128)}, f32[1536,512]{0,1:T(8,128)}), (f32[1536,512]{0,1:T(8,128)}, f32[1536,512]{0,1:T(8,128)})) %all-reduce.3.cloned.1.call-update) | async-done | bytes 6291472 | tf_op jit(solution)/shard_map/psum | solution.py:108
  282.2 2.2 multiply_convert_fusion.1
  284.5 1.6 copy.101
  286.0 2.2 multiply_convert_fusion
  288.3 1.6 copy.102
  (39 shorter events, 0.3 us)
Async XLA Ops:
  7.2 102.5 %all-gather.8.cloned.1.call-start = ((), (), s32[]{:S(2)}) async-start(), calls=%async_computation.2 | async-start | bytes 1310720 | tf_op jit(solution)/shard_map/all_gather | solution.py:41
  8.2 10.0 %copy-start.5 = (f32[128,4]{1,0:T(8,128)}, f32[128,4]{1,0:T(8,128)S(1)}, u32[]{:S(2)}) copy-start(f32[128,4]{1,0:T(8,128)S(1)} %reduce_window_sum.22) | copy-start | bytes 6148
  10.4 99.0 %copy-start.2 = (bf16[1,128,512]{1,2,0:T(8,128)(2,1)}, bf16[1,128,512]{1,2,0:T(8,128)(2,1)S(1)}, u32[]{:S(2)}) copy-start(bf16[1,128,512]{1,2,0:T(8,128)(2,1)S(1)} %copy.119) | copy-start | bytes 393220
  56.8 6.5 %copy-start.11 = (bf16[1,128,512]{2,1,0:T(8,128)(2,1)S(1)}, bf16[1,128,512]{2,1,0:T(8,128)(2,1)}, u32[]{:S(2)}) copy-start(bf16[1,128,512]{2,1,0:T(8,128)(2,1)} %param.9) | copy-start | bytes 393220
  56.8 6.6 %copy-start.12 = (bf16[1,128,512]{2,1,0:T(8,128)(2,1)S(1)}, bf16[1,128,512]{2,1,0:T(8,128)(2,1)}, u32[]{:S(2)}) copy-start(bf16[1,128,512]{2,1,0:T(8,128)(2,1)} %param.8) | copy-start | bytes 393220
  56.8 52.3 %copy-start.6 = (f32[128,4]{1,0:T(8,128)S(1)}, f32[128,4]{1,0:T(8,128)}, u32[]{:S(2)}) copy-start(f32[128,4]{1,0:T(8,128)} %copy-done.5) | copy-start | bytes 6148
  56.8 94.0 %all-to-all-start = ((bf16[4,2,98304]{2,1,0:T(2,128)(2,1)}), bf16[4,2,98304]{2,1,0:T(2,128)(2,1)}, u32[]{:S(2)}, u32[]{:S(2)}) async-start(bf16[4,2,98304]{2,1,0:T(2,128)(2,1)} %reshape.75), calls=%async_computation | async-start | bytes 3145728 | tf_op jit(solution)/shard_map/all_to_all | solution.py:92
  63.3 101.6 %all-gather.6.cloned.1.call-start = ((), (), s32[]{:S(2)}) async-start(), calls=%async_computation.1 | async-start | bytes 1310720 | tf_op jit(solution)/shard_map/all_gather | solution.py:40
  64.4 217.8 %all-reduce.3.cloned.1.call-start = ((), (), s32[]{:S(2)}) async-start(), calls=%async_computation.3 | async-start | bytes 12582912 | tf_op jit(solution)/shard_map/psum | solution.py:108
  109.6 25.9 %copy-start.9 = (bf16[4,128,128]{2,1,0:T(8,128)(2,1)}, bf16[4,128,128]{2,1,0:T(8,128)(2,1)S(1)}, u32[]{:S(2)}) copy-start(bf16[4,128,128]{2,1,0:T(8,128)(2,1)S(1)} %fusion.12) | copy-start | bytes 393220
  111.1 24.7 %copy-start.3 = (bf16[1,128,512]{1,2,0:T(8,128)(2,1)S(1)}, bf16[1,128,512]{1,2,0:T(8,128)(2,1)}, u32[]{:S(2)}) copy-start(bf16[1,128,512]{1,2,0:T(8,128)(2,1)} %copy-done.2) | copy-start | bytes 393220
  136.1 14.7 %copy-start.7 = (bf16[128,4,128]{0,2,1:T(8,128)(2,1)}, bf16[128,4,128]{0,2,1:T(8,128)(2,1)S(1)}, u32[]{:S(2)}) copy-start(bf16[128,4,128]{0,2,1:T(8,128)(2,1)S(1)} %fusion.11) | copy-start | bytes 393220
  155.2 1.8 copy-start.1
  157.0 2.6 copy-start
  162.3 0.9 copy-start.10
  162.3 1.1 copy-start.8
  162.3 6.2 %copy-start.4 = (bf16[1,128,512]{1,2,0:T(8,128)(2,1)S(1)}, bf16[1,128,512]{1,2,0:T(8,128)(2,1)}, u32[]{:S(2)}) copy-start(bf16[1,128,512]{1,2,0:T(8,128)(2,1)} %copy-done.2) | copy-start | bytes 393220
Sparse Core Ops, SparseCore 0:
  11.4 30.6 all-gather.7
  65.7 45.5 all-gather.5
  162.4 119.7 all-reduce.2
where the time goes:
time: 297 us; the launch traced here: 296 us
  waiting for transfers between devices  113 us (38%)
  blocking collectives  83.2 us (28%)
  other arithmetic  40.7 us (14%)
  local copies, waits for them, and re-layouts  26.9 us (9%)
  between operations  14 us (5%)
  matrix products  12.2 us (4%)
  starting transfers between devices  6.54 us (2%)
    psum x1, waiting for transfers between devices, per_device(): key_summed, value_summed = lax.psum((key_part, value_part), 'dp')  113 us
    all_gather x1, blocking collectives, per_device(): lax.all_gather(totals[None], 'seq', axis=0, tiled=True)  44.7 us
    unnamed x3, other arithmetic  35.9 us
    all_gather x1, blocking collectives, per_device(): lax.all_gather(grad_key, 'seq', axis=1, tiled=True)[0]  23.9 us
    unnamed x38, local copies, waits for them, and re-layouts  22.8 us
    all_gather x1, blocking collectives, per_device(): lax.all_gather(grad_value, 'seq', axis=1, tiled=True)[0]  14.7 us
    all_to_all x1, starting transfers between devices, per_device(): lax.all_to_all(layer_input, 'seq', split_axis=2, concat_axis=1, tiled=True)  6.46 us
  transfers between devices with their start and end apart: 4, of which 1 were waited for; matrix products, arithmetic and copies ran while one was open for 23% of the time, Pallas kernels for 0%

commit v1 on v0

v1 whole, which is shorter than its diff:
```python
import functools
import math

import jax
import jax.numpy as jnp
from jax import lax
from jax.experimental import pallas as pl
from jax.experimental.pallas import tpu as pltpu
from jax.sharding import PartitionSpec as P

DH = 128
CHUNKS = 2
MESH = pl.DeviceIdType.MESH
BF16 = jnp.bfloat16
F32 = jnp.float32


def dot(left, right, dims):
    return lax.dot_general(left, right, (dims, ((), ())), preferred_element_type=F32)


NN = ((1,), (0,))
NT = ((1,), (1,))
TN = ((0,), (0,))


def kernel(
    n, bits, heads, factor,
    x_hbm, q_ref, k_ref, v_ref, g_ref, ld_ref,
    gq_ref, gk_ref, gv_ref, ok_ref, ov_ref,
    cum_s, tot_s, kst_own, qst_own, kst, qst, tot_b, tot_a, w_b, w_a, pre, suf,
    acc_q, acc_k, acc_v, rx, rxt, gg, half_send, half_recv, mine, lev_send, lev_recv,
    st_send, st_recv, x_send, x_recv, x_sem, g_send, g_recv,
    c_send, c_recv, l_send, l_recv, f_send, f_recv,
):
    s = lax.axis_index("seq")
    d = lax.axis_index("dp")
    length = q_ref.shape[0]
    cols = rx.shape[2]
    half = cols // 2
    size = half // CHUNKS
    outs = (ok_ref, ov_ref)

    def partner(bit):
        block = 1 << bit
        low = lax.rem(lax.div(d, block), 2)
        return d + block - 2 * block * low

    near = partner(0)
    barrier = pltpu.get_barrier_semaphore()
    for step in range(1, n):
        pl.semaphore_signal(
            barrier, inc=1, device_id={"seq": lax.rem(s + step, n)}, device_id_type=MESH
        )
    for bit in range(bits):
        pl.semaphore_signal(barrier, inc=1, device_id={"dp": partner(bit)}, device_id_type=MESH)

    row = lax.broadcasted_iota(jnp.int32, (length, length), 0)
    col = lax.broadcasted_iota(jnp.int32, (length, length), 1)
    lower = row >= col
    tri = jnp.where(lower, 1.0, 0.0).astype(F32)
    tot_s[...] = jnp.zeros_like(tot_s)
    for h in range(heads):
        at = pl.ds(h * DH, DH)
        decays = jnp.broadcast_to(ld_ref[:, h : h + 1], (length, DH))
        cum = lax.dot_general(
            tri, decays, (NN, ((), ())), precision=lax.Precision.HIGHEST, preferred_element_type=F32
        )
        cum_s[h] = cum
        total = cum[length - 1 : length, :]
        tot_s[h : h + 1, :] = total
        keys = (k_ref[:, at].astype(F32) * jnp.exp(total - cum)).astype(BF16)
        queries = (q_ref[:, at].astype(F32) * jnp.exp(cum)).astype(BF16)
        kst_own[h] = dot(keys, v_ref[:, at], TN).astype(BF16)
        qst_own[h] = dot(queries, g_ref[:, at], TN).astype(BF16)

    pl.semaphore_wait(barrier, n - 1 + bits)

    def send(kind, step, src, dst, peer):
        return pltpu.make_async_remote_copy(
            src_ref=src, dst_ref=dst, send_sem=st_send.at[kind, step - 1],
            recv_sem=st_recv.at[kind, step - 1], device_id={"seq": peer}, device_id_type=MESH,
        )

    def forward(step):
        peer = lax.rem(s + step, n)
        return (
            send(0, step, tot_s, tot_b.at[step - 1], peer),
            send(1, step, kst_own, kst.at[step - 1], peer),
        )

    def backward(step):
        peer = lax.rem(s + n - step, n)
        return (
            send(2, step, tot_s, tot_a.at[step - 1], peer),
            send(3, step, qst_own, qst.at[step - 1], peer),
        )

    for step in range(n - 1, 0, -1):
        @pl.when(s + step < n)
        def _(step=step):
            for copy in forward(step):
                copy.start()

        @pl.when(s >= step)
        def _(step=step):
            for copy in backward(step):
                copy.start()

    x_own = pltpu.make_async_copy(
        x_hbm.at[:, pl.ds(pl.multiple_of(s * cols, 128), cols)], rx.at[0], x_sem
    )
    x_own.start()
    x_copies = []
    for step in range(1, n):
        peer = lax.rem(s + step, n)
        copy = pltpu.make_async_remote_copy(
            src_ref=x_hbm.at[:, pl.ds(pl.multiple_of(peer * cols, 128), cols)],
            dst_ref=rx.at[step], send_sem=x_send.at[step - 1], recv_sem=x_recv.at[step - 1],
            device_id={"seq": peer}, device_id_type=MESH,
        )
        copy.start()
        x_copies.append(copy)

    for h in range(heads):
        at = pl.ds(h * DH, DH)
        cum = cum_s[h]
        mask = jnp.where(lower, jnp.exp(jnp.minimum(cum - cum.T, 0.0)), 0.0)
        q, k, v, g = q_ref[:, at], k_ref[:, at], v_ref[:, at], g_ref[:, at]
        value_weights = (dot(g, v, NT) * mask).astype(BF16)
        key_weights = (dot(q, k, NT) * mask).astype(BF16)
        acc_q[:, at] = dot(value_weights, k, NN)
        acc_k[:, at] = dot(value_weights, q, TN)
        acc_v[:, at] = dot(key_weights, g, TN)

    for ref in (pre, suf, w_b, w_a):
        ref[...] = jnp.zeros_like(ref)
    for step in range(1, n):
        @pl.when(s + step < n)
        def _(step=step):
            for copy in backward(step):
                copy.wait_recv()
            weight = jnp.exp(w_a[...])
            for h in range(heads):
                suf[h] += weight[h : h + 1, :] * qst[step - 1, h].astype(F32)
            w_a[...] += tot_a[step - 1]

        @pl.when(s >= step)
        def _(step=step):
            for copy in forward(step):
                copy.wait_recv()
            weight = jnp.exp(w_b[...])
            for h in range(heads):
                pre[h] += weight[h : h + 1, :] * kst[step - 1, h].astype(F32)
            w_b[...] += tot_b[step - 1]

    scale = 1.0 / DH
    g_copies = []

    def spread(part):
        copies = []
        for step in range(n - 1, 0, -1):
            copy = pltpu.make_async_remote_copy(
                src_ref=gg.at[part, 0], dst_ref=gg.at[part, step],
                send_sem=g_send.at[part, step - 1], recv_sem=g_recv.at[part, step - 1],
                device_id={"seq": lax.rem(s + step, n)}, device_id_type=MESH,
            )
            copy.start()
            copies.append(copy)
        g_copies.append(copies)

    for h in range(heads):
        at = pl.ds(h * DH, DH)
        cum = cum_s[h]
        to_end = jnp.exp(cum[length - 1 : length, :] - cum)
        carried = to_end * dot(v_ref[:, at], suf[h].astype(BF16), NT)
        gg[0, 0, :, at] = ((acc_k[:, at] + carried) * scale).astype(BF16)
    spread(0)
    for h in range(heads):
        at = pl.ds(h * DH, DH)
        cum = cum_s[h]
        to_end = jnp.exp(cum[length - 1 : length, :] - cum)
        carried = to_end * dot(k_ref[:, at], suf[h].astype(BF16), NN)
        gg[1, 0, :, at] = ((acc_v[:, at] + carried) * scale).astype(BF16)
    spread(1)
    for h in range(heads):
        at = pl.ds(h * DH, DH)
        carried = jnp.exp(cum_s[h]) * dot(g_ref[:, at], pre[h].astype(BF16), NT)
        gq_ref[:, at] = ((acc_q[:, at] + carried) * scale).astype(BF16)
    gk_ref[...] = gg[0, 0]
    gv_ref[...] = gg[1, 0]

    for step in range(n):
        if step == 0:
            x_own.wait()
        else:
            x_copies[step - 1].wait_recv()
        rxt[:, step * length : (step + 1) * length] = rx[step].T

    low = lax.rem(d, 2)
    own_row = low * half
    far_row = (1 - low) * half

    def product(start, part):
        rows = rxt[pl.ds(pl.multiple_of(start, 16), size), :]
        return dot(rows, gg[part].reshape(n * length, gg.shape[3]), NN)

    def exchange(src, dst, send_sem, recv_sem, to):
        return pltpu.make_async_remote_copy(
            src_ref=src, dst_ref=dst, send_sem=send_sem, recv_sem=recv_sem,
            device_id={"dp": to}, device_id_type=MESH,
        )

    halves, levels, finals = {}, {}, {}
    for part in range(2):
        for copy in g_copies[part]:
            copy.wait_recv()
        for i in range(CHUNKS):
            half_send[part, i] = product(far_row + i * size, part).astype(BF16)
            halves[part, i] = exchange(
                half_send.at[part, i], half_recv.at[part, i],
                c_send.at[part, i], c_recv.at[part, i], near,
            )
            halves[part, i].start()
        for i in range(CHUNKS):
            total = product(own_row + i * size, part)
            halves[part, i].wait_recv()
            total = total + half_recv[part, i].astype(F32)
            lev_send[0, part, i] = total.astype(BF16)
            levels[0, part, i] = exchange(
                lev_send.at[0, part, i], lev_recv.at[0, part, i],
                l_send.at[0, part, i], l_recv.at[0, part, i], partner(1),
            )
            levels[0, part, i].start()
    for level in range(bits - 1):
        for part in range(2):
            for i in range(CHUNKS):
                levels[level, part, i].wait_recv()
                total = lev_send[level, part, i].astype(F32) + lev_recv[level, part, i].astype(F32)
                if level < bits - 2:
                    lev_send[level + 1, part, i] = total.astype(BF16)
                    levels[level + 1, part, i] = exchange(
                        lev_send.at[level + 1, part, i], lev_recv.at[level + 1, part, i],
                        l_send.at[level + 1, part, i], l_recv.at[level + 1, part, i],
                        partner(level + 2),
                    )
                    levels[level + 1, part, i].start()
                    continue
                here = outs[part].at[pl.ds(pl.multiple_of(own_row + i * size, 16), size), :]
                here[...] = (total * factor).astype(BF16)
                finals[part, i] = exchange(
                    here, here, f_send.at[part, i], f_recv.at[part, i], near
                )
                finals[part, i].start()

    for step in range(1, n):
        @pl.when(s + step < n)
        def _(step=step):
            for copy in forward(step):
                copy.wait_send()

        @pl.when(s >= step)
        def _(step=step):
            for copy in backward(step):
                copy.wait_send()
    for copy in x_copies + g_copies[0] + g_copies[1] + list(halves.values()) + list(levels.values()):
        copy.wait_send()
    for copy in finals.values():
        copy.wait()


def per_device(layer_input, queries, key_rows, value_rows, grad_out, log_decay):
    n = lax.axis_size("seq")
    dp = lax.axis_size("dp")
    bits = dp.bit_length() - 1
    length, width = queries.shape[1:]
    heads = log_decay.shape[2]
    features = layer_input.shape[2]
    cols = features // n
    size = cols // 2 // CHUNKS
    tot_rows = -(-heads // 8) * 8
    factor = 1.0 / math.sqrt(dp * n * length)
    vmem = pl.BlockSpec(memory_space=pltpu.VMEM)
    dma = pltpu.SemaphoreType.DMA
    tile = (heads, DH, DH)
    grads = pl.pallas_call(
        functools.partial(kernel, n, bits, heads, factor),
        out_shape=[jax.ShapeDtypeStruct((length, width), BF16)] * 3
        + [jax.ShapeDtypeStruct((cols, width), BF16)] * 2,
        in_specs=[pl.BlockSpec(memory_space=pl.ANY)] + [vmem] * 5,
        out_specs=[vmem] * 5,
        scratch_shapes=[
            pltpu.VMEM((heads, length, DH), F32),
            pltpu.VMEM((tot_rows, DH), F32),
            pltpu.VMEM(tile, BF16),
            pltpu.VMEM(tile, BF16),
            pltpu.VMEM((n - 1,) + tile, BF16),
            pltpu.VMEM((n - 1,) + tile, BF16),
            pltpu.VMEM((n - 1, tot_rows, DH), F32),
            pltpu.VMEM((n - 1, tot_rows, DH), F32),
            pltpu.VMEM((tot_rows, DH), F32),
            pltpu.VMEM((tot_rows, DH), F32),
            pltpu.VMEM(tile, F32),
            pltpu.VMEM(tile, F32),
            pltpu.VMEM((length, width), F32),
            pltpu.VMEM((length, width), F32),
            pltpu.VMEM((length, width), F32),
            pltpu.VMEM((n, length, cols), BF16),
            pltpu.VMEM((cols, n * length), BF16),
            pltpu.VMEM((2, n, length, width), BF16),
            pltpu.VMEM((2, CHUNKS, size, width), BF16),
            pltpu.VMEM((2, CHUNKS, size, width), BF16),
            pltpu.VMEM((8, 128), F32),
            pltpu.VMEM((bits - 1, 2, CHUNKS, size, width), BF16),
            pltpu.VMEM((bits - 1, 2, CHUNKS, size, width), BF16),
            dma((4, n - 1)), dma((4, n - 1)),
            dma((n - 1,)), dma((n - 1,)), dma,
            dma((2, n - 1)), dma((2, n - 1)),
            dma((2, CHUNKS)), dma((2, CHUNKS)),
            dma((bits - 1, 2, CHUNKS)), dma((bits - 1, 2, CHUNKS)),
            dma((2, CHUNKS)), dma((2, CHUNKS)),
        ],
        compiler_params=pltpu.CompilerParams(
            collective_id=0, has_side_effects=True, vmem_limit_bytes=48 << 20
        ),
    )(layer_input[0], queries[0], key_rows[0], value_rows[0], grad_out[0], log_decay[0])
    return (grads[0][None], grads[1][None], grads[2][None], grads[3], grads[4])


def solution(mesh):
    return jax.shard_map(
        per_device,
        mesh=mesh,
        in_specs=(
            P("dp", "seq", None),
            P("dp", "seq", "head"),
            P("dp", "seq", "head"),
            P("dp", "seq", "head"),
            P("dp", "seq", "head"),
            P("dp", "seq", "head"),
        ),
        out_specs=(
            P("dp", "seq", "head"),
            P("dp", "seq", "head"),
            P("dp", "seq", "head"),
            P("seq", "head"),
            P("seq", "head"),
        ),
        check_vma=False,
    )
```

time: 297 us -> 120 us (0.40)
  waiting for transfers between devices: 113 us -> 0 us
  Pallas kernels: 0 us -> 109 us
  blocking collectives: 83.2 us -> 0 us
  other arithmetic: 40.7 us -> 0 us
  local copies, waits for them, and re-layouts: 26.9 us -> 10.1 us
  between operations: 14 us -> 0.65 us
  matrix products: 12.2 us -> 0 us
  starting transfers between devices: 6.54 us -> 0 us
    psum x1 -> x0, waiting for transfers between devices: 113 us -> none  [per_device(): key_summed, value_summed = lax.psum((key_part, value_part), 'dp')]
    pallas_call x0 -> x1, Pallas kernels: none -> 109 us  [per_device(): pl.pallas_call(functools.partial(kernel, n, bits, heads, factor), out_sha...]
    all_gather x3 -> x0, blocking collectives: 83.2 us -> none  [the longest x1 44.7 us: per_device(): lax.all_gather(totals[None], 'seq', axis=0, tiled=True)]
    unnamed x3 -> x0, other arithmetic: 35.9 us -> none
    unnamed x38 -> x16, local copies, waits for them, and re-layouts: 22.8 us -> 10.1 us
    dot_general x12 -> x0, matrix products: 12.2 us -> none  [the longest x1 3.56 us: per_device(): jnp.einsum('cp,cpqt->pqt', leading_weight, every_key_row, precision=top_p...]
    all_to_all x1 -> x0, starting transfers between devices: 6.46 us -> none  [per_device(): lax.all_to_all(layer_input, 'seq', split_axis=2, concat_axis=1, tiled=True)]
    convert_element_type x2 -> x0, other arithmetic: 4.5 us -> none  [the longest x1 2.25 us: per_device(): key_weight_grad = (key_summed * factor).astype(jnp.bfloat16)]
  transfers between devices with their start and end apart: 4 -> 0, of which waited for: 1 -> 0; matrix products, arithmetic and copies ran while one was open for 23% -> 0% of each run, Pallas kernels for 0% -> 0%
where the time goes in v1:
time: 120 us
  Pallas kernels  109 us (91%)
  local copies, waits for them, and re-layouts  10.1 us (8%)
    pallas_call x1, Pallas kernels, per_device(): pl.pallas_call(functools.partial(kernel, n, bits, heads, factor), out_sha...  109 us
    unnamed x16, local copies, waits for them, and re-layouts  10.1 us

profile of v1, /device:TPU:0, one launch (start us, length us, event | category | flops | bytes accessed | tf_op | source)
XLA Modules:
  0.0 119.7 jit_solution(6518536779269437646)
XLA Ops:
  0.6 0.8 copy.11
  1.4 0.0 copy-start
  1.4 1.4 %copy-done = bf16[1,128,6144]{2,1,0:T(8,128)(2,1)S(1)} copy-done((bf16[1,128,6144]{2,1,0:T(8,128)(2,1)S(1)}, bf16[1,128,6144]{2,1,0:T(8,128)(2,1)}, u32[]{:S(2)}) %copy-start) | copy-done | bytes 1572888
  2.8 0.0 copy-start.1
  2.8 0.9 copy-done.1
  3.7 0.0 copy-start.2
  3.7 0.9 copy-done.2
  4.6 0.0 copy-start.3
  4.6 0.9 copy-done.3
  5.5 0.0 copy-start.4
  5.5 0.9 copy-done.4
  6.4 109.0 %shard_map.101 = (bf16[128,512]{1,0:T(8,128)(2,1)S(1)}, bf16[128,512]{1,0:T(8,128)(2,1)S(1)}, bf16[128,512]{1,0:T(8,128)(2,1)S(1)}, bf16[1536,512]{1,0:T(8,128)(2,1)S(1)}, bf16[1536,512]{1,0:T(8,128)(2,1)S(1)}) custom-call(bf16[128,6144]{1,0:T(8,128)(2,1)S(1)} %bitcast.9, bf16[128,512]{1,0:T(8,128)(2,1)S(1)} %bitcast.11, bf16[128,512]{1,0:T(8,128)(2,1)S(1)} %bitcast.12, ...), custom_call_target="tpu_custom_call" | custom-call | tf_op jit(solution)/shard_map/pallas_call | solution.py:286
  115.5 0.7 copy.17
  116.1 0.7 copy.18
  116.8 0.7 copy.19
  117.4 1.1 copy.20
  118.6 1.1 copy.21
Async XLA Ops:
  1.4 1.4 %copy-start = (bf16[1,128,6144]{2,1,0:T(8,128)(2,1)S(1)}, bf16[1,128,6144]{2,1,0:T(8,128)(2,1)}, u32[]{:S(2)}) copy-start(bf16[1,128,6144]{2,1,0:T(8,128)(2,1)} %param.6) | copy-start | bytes 4718596
  2.8 0.9 copy-start.1
  3.7 0.9 copy-start.2
  4.6 0.9 copy-start.3
  5.5 0.9 copy-start.4

commit v2 on v1

v2 whole, which is shorter than its diff:
```python
import functools
import math

import jax
import jax.numpy as jnp
from jax import lax
from jax.experimental import pallas as pl
from jax.experimental.pallas import tpu as pltpu
from jax.sharding import PartitionSpec as P

DH = 128
CHUNKS = 2
GROUPS = 2
PIECES = 3
MESH = pl.DeviceIdType.MESH
BF16 = jnp.bfloat16
F32 = jnp.float32


def dot(left, right, dims):
    return lax.dot_general(left, right, (dims, ((), ())), preferred_element_type=F32)


NN = ((1,), (0,))
NT = ((1,), (1,))
TN = ((0,), (0,))


def kernel(
    n, bits, heads, factor,
    x_hbm, q_hbm, k_hbm, v_hbm, g_hbm, ld_ref,
    gq_ref, gk_ref, gv_ref, ok_ref, ov_ref,
    q_ref, k_ref, v_ref, g_ref,
    cum_s, tot_s, kst_own, qst_own, kst, qst, tot_b, tot_a, w_b, w_a, pre, suf,
    acc_q, acc_k, acc_v, rx, rxt, gg, half_send, half_recv, lev_send, lev_recv,
    in_sem, st_send, st_recv, x_send, x_recv, xf_send, xf_recv, x_sem, g_send, g_recv,
    c_send, c_recv, l_send, l_recv, f_send, f_recv,
):
    s = lax.axis_index("seq")
    d = lax.axis_index("dp")
    head = lax.axis_index("head")
    length = q_ref.shape[0]
    cols = rx.shape[2]
    half = cols // 2
    size = half // CHUNKS
    piece = cols // PIECES
    group = heads // GROUPS
    parts = 2 * GROUPS
    wide = gg.shape[3]
    outs = (ok_ref, ov_ref)

    def partner(bit):
        block = 1 << bit
        low = lax.rem(lax.div(d, block), 2)
        return d + block - 2 * block * low

    near = partner(0)
    side = lax.rem(head, 2)
    mate = head + 1 - 2 * side
    loads = [
        pltpu.make_async_copy(src, dst, in_sem.at[i])
        for i, (src, dst) in enumerate(
            ((q_hbm, q_ref), (g_hbm, g_ref), (k_hbm, k_ref), (v_hbm, v_ref))
        )
    ]
    for copy in loads:
        copy.start()
    barrier = pltpu.get_barrier_semaphore()
    for step in range(1, n):
        pl.semaphore_signal(
            barrier, inc=1, device_id={"seq": lax.rem(s + step, n)}, device_id_type=MESH
        )
    for bit in range(bits):
        pl.semaphore_signal(barrier, inc=1, device_id={"dp": partner(bit)}, device_id_type=MESH)
    pl.semaphore_signal(barrier, inc=1, device_id={"head": mate}, device_id_type=MESH)
    x_own = pltpu.make_async_copy(
        x_hbm.at[:, pl.ds(pl.multiple_of(s * cols, 128), cols)], rx.at[0], x_sem
    )
    x_own.start()
    pl.semaphore_wait(barrier, n + bits)

    strip = pl.ds(pl.multiple_of(side * (length // 2), 16), length // 2)
    x_copies, x_swaps = {}, {}

    def x_start(i):
        for step in range(n - 1, 0, -1):
            peer = lax.rem(s + step, n)
            x_copies[i, step] = pltpu.make_async_remote_copy(
                src_ref=x_hbm.at[strip, pl.ds(pl.multiple_of(peer * cols + i * piece, 128), piece)],
                dst_ref=rx.at[step, strip, pl.ds(i * piece, piece)],
                send_sem=x_send.at[i, step - 1], recv_sem=x_recv.at[i, step - 1],
                device_id={"seq": peer}, device_id_type=MESH,
            )
            x_copies[i, step].start()

    def x_swap(i):
        for step in range(1, n):
            x_copies[i, step].wait_recv()
            here = rx.at[step, strip, pl.ds(i * piece, piece)]
            x_swaps[i, step] = pltpu.make_async_remote_copy(
                src_ref=here, dst_ref=here,
                send_sem=xf_send.at[i, step - 1], recv_sem=xf_recv.at[i, step - 1],
                device_id={"head": mate}, device_id_type=MESH,
            )
            x_swaps[i, step].start()

    def x_turn(i):
        for step in range(n):
            if step:
                x_swaps[i, step].wait_recv()
            rxt[i * piece : (i + 1) * piece, step * length : (step + 1) * length] = rx[
                step, :, i * piece : (i + 1) * piece
            ].T

    x_start(0)

    row = lax.broadcasted_iota(jnp.int32, (length, length), 0)
    col = lax.broadcasted_iota(jnp.int32, (length, length), 1)
    lower = row >= col
    tri = jnp.where(lower, 1.0, 0.0).astype(F32)
    tot_s[...] = jnp.zeros_like(tot_s)
    loads[0].wait()
    loads[1].wait()
    for h in range(heads):
        at = pl.ds(h * DH, DH)
        decays = jnp.broadcast_to(ld_ref[:, h : h + 1], (length, DH))
        cum = lax.dot_general(
            tri, decays, (NN, ((), ())), precision=lax.Precision.HIGHEST, preferred_element_type=F32
        )
        cum_s[h] = cum
        tot_s[h : h + 1, :] = cum[length - 1 : length, :]
        queries = (q_ref[:, at].astype(F32) * jnp.exp(cum)).astype(BF16)
        qst_own[h] = dot(queries, g_ref[:, at], TN).astype(BF16)

    def send(kind, step, src, dst, peer):
        return pltpu.make_async_remote_copy(
            src_ref=src, dst_ref=dst, send_sem=st_send.at[kind, step - 1],
            recv_sem=st_recv.at[kind, step - 1], device_id={"seq": peer}, device_id_type=MESH,
        )

    def forward(step):
        peer = lax.rem(s + step, n)
        return (
            send(0, step, tot_s, tot_b.at[step - 1], peer),
            send(1, step, kst_own, kst.at[step - 1], peer),
        )

    def backward(step):
        peer = lax.rem(s + n - step, n)
        return (
            send(2, step, tot_s, tot_a.at[step - 1], peer),
            send(3, step, qst_own, qst.at[step - 1], peer),
        )

    for step in range(n - 1, 0, -1):
        @pl.when(s >= step)
        def _(step=step):
            for copy in backward(step):
                copy.start()

    loads[2].wait()
    loads[3].wait()
    for h in range(heads):
        at = pl.ds(h * DH, DH)
        cum = cum_s[h]
        to_end = jnp.exp(cum[length - 1 : length, :] - cum)
        keys = (k_ref[:, at].astype(F32) * to_end).astype(BF16)
        kst_own[h] = dot(keys, v_ref[:, at], TN).astype(BF16)
    for i in range(1, PIECES):
        x_start(i)
    for step in range(n - 1, 0, -1):
        @pl.when(s + step < n)
        def _(step=step):
            for copy in forward(step):
                copy.start()

    for h in range(heads):
        at = pl.ds(h * DH, DH)
        cum = cum_s[h]
        mask = jnp.where(lower, jnp.exp(jnp.minimum(cum - cum.T, 0.0)), 0.0)
        q, k, v, g = q_ref[:, at], k_ref[:, at], v_ref[:, at], g_ref[:, at]
        value_weights = (dot(g, v, NT) * mask).astype(BF16)
        key_weights = (dot(q, k, NT) * mask).astype(BF16)
        acc_q[:, at] = dot(value_weights, k, NN)
        acc_k[:, at] = dot(value_weights, q, TN)
        acc_v[:, at] = dot(key_weights, g, TN)

    x_swap(0)

    for ref in (pre, suf, w_b, w_a):
        ref[...] = jnp.zeros_like(ref)
    for step in range(1, n):
        @pl.when(s + step < n)
        def _(step=step):
            for copy in backward(step):
                copy.wait_recv()
            weight = jnp.exp(w_a[...])
            for h in range(heads):
                suf[h] += weight[h : h + 1, :] * qst[step - 1, h].astype(F32)
            w_a[...] += tot_a[step - 1]

    scale = 1.0 / DH

    def relay(way, part, hop):
        step = 1 if way == 0 else n - 1
        have = hop if way == 0 else (n - hop) % n
        give = hop + 1 if way == 0 else n - hop - 1
        return pltpu.make_async_remote_copy(
            src_ref=gg.at[part, have], dst_ref=gg.at[part, give],
            send_sem=g_send.at[way, part, hop], recv_sem=g_recv.at[way, part, hop],
            device_id={"seq": lax.rem(s + step, n)}, device_id_type=MESH,
        )

    def sends(way, hop):
        if way == 0:
            return jnp.logical_and(s >= hop, s + 1 < n)
        return jnp.logical_and(s + hop < n, s >= 1)

    def gets(way, hop):
        return s >= hop + 1 if way == 0 else s + hop + 1 < n

    def pass_on(part, hop):
        for way in range(2):
            @pl.when(gets(way, hop))
            def _(way=way):
                relay(way, part, hop).wait_recv()

            if hop + 1 < n - 1:
                @pl.when(sends(way, hop + 1))
                def _(way=way):
                    relay(way, part, hop + 1).start()

    for part in range(parts):
        for i in range(group):
            h = (part % GROUPS) * group + i
            at = pl.ds(h * DH, DH)
            cum = cum_s[h]
            to_end = jnp.exp(cum[length - 1 : length, :] - cum)
            low_suffix = suf[h].astype(BF16)
            if part < GROUPS:
                carried = to_end * dot(v_ref[:, at], low_suffix, NT)
                result = ((acc_k[:, at] + carried) * scale).astype(BF16)
                gk_ref[:, at] = result
            else:
                carried = to_end * dot(k_ref[:, at], low_suffix, NN)
                result = ((acc_v[:, at] + carried) * scale).astype(BF16)
                gv_ref[:, at] = result
            gg[part, 0, :, i * DH : (i + 1) * DH] = result
        for way in range(2):
            @pl.when(sends(way, 0))
            def _(way=way, part=part):
                relay(way, part, 0).start()

    low = lax.rem(d, 2)
    own_row = low * half
    far_row = (1 - low) * half

    def product(start, part):
        rows = rxt[pl.ds(pl.multiple_of(start, 16), size), :]
        return dot(rows, gg[part].reshape(n * length, wide), NN)

    def exchange(src, dst, send_sem, recv_sem, to):
        return pltpu.make_async_remote_copy(
            src_ref=src, dst_ref=dst, send_sem=send_sem, recv_sem=recv_sem,
            device_id={"dp": to}, device_id_type=MESH,
        )

    def level_up(level, part, i):
        levels[level, part, i] = exchange(
            lev_send.at[level, part, i], lev_recv.at[level, part, i],
            l_send.at[level, part, i], l_recv.at[level, part, i], partner(level + 1),
        )
        levels[level, part, i].start()

    halves, levels, finals = {}, {}, {}

    def multiply(part):
        for i in range(CHUNKS):
            half_send[part, i] = product(far_row + i * size, part).astype(BF16)
            halves[part, i] = exchange(
                half_send.at[part, i], half_recv.at[part, i],
                c_send.at[part, i], c_recv.at[part, i], near,
            )
            halves[part, i].start()
        for i in range(CHUNKS):
            total = product(own_row + i * size, part)
            halves[part, i].wait_recv()
            total = total + half_recv[part, i].astype(F32)
            lev_send[0, part, i] = total.astype(BF16)
            level_up(0, part, i)

    pass_on(0, 0)
    for i in range(1, PIECES):
        x_swap(i)
    x_own.wait()
    x_turn(0)
    for wave in range(1, parts + n - 2):
        for part in range(parts):
            if 0 <= wave - part < n - 1:
                pass_on(part, wave - part)
        if wave <= n - 2:
            for i in range(1, PIECES):
                if (i - 1) * (n - 2) // (PIECES - 1) == wave - 1:
                    x_turn(i)
        if wave >= n - 2:
            multiply(wave - (n - 2))

    for step in range(1, n):
        @pl.when(s >= step)
        def _(step=step):
            for copy in forward(step):
                copy.wait_recv()
            weight = jnp.exp(w_b[...])
            for h in range(heads):
                pre[h] += weight[h : h + 1, :] * kst[step - 1, h].astype(F32)
            w_b[...] += tot_b[step - 1]
    for h in range(heads):
        at = pl.ds(h * DH, DH)
        carried = jnp.exp(cum_s[h]) * dot(g_ref[:, at], pre[h].astype(BF16), NT)
        gq_ref[:, at] = ((acc_q[:, at] + carried) * scale).astype(BF16)

    for level in range(bits - 1):
        for part in range(parts):
            for i in range(CHUNKS):
                levels[level, part, i].wait_recv()
                total = lev_send[level, part, i].astype(F32) + lev_recv[level, part, i].astype(F32)
                if level < bits - 2:
                    lev_send[level + 1, part, i] = total.astype(BF16)
                    level_up(level + 1, part, i)
                    continue
                here = outs[part // GROUPS].at[
                    pl.ds(pl.multiple_of(own_row + i * size, 16), size),
                    pl.ds((part % GROUPS) * wide, wide),
                ]
                here[...] = (total * factor).astype(BF16)
                finals[part, i] = exchange(
                    here, here, f_send.at[part, i], f_recv.at[part, i], near
                )
                finals[part, i].start()

    for step in range(1, n):
        @pl.when(s + step < n)
        def _(step=step):
            for copy in forward(step):
                copy.wait_send()

        @pl.when(s >= step)
        def _(step=step):
            for copy in backward(step):
                copy.wait_send()
    for hop in range(n - 1):
        for way in range(2):
            @pl.when(sends(way, hop))
            def _(way=way, hop=hop):
                for part in range(parts):
                    relay(way, part, hop).wait_send()
    for copies in (x_copies, x_swaps, halves, levels):
        for copy in copies.values():
            copy.wait_send()
    for copy in finals.values():
        copy.wait()


def per_device(layer_input, queries, key_rows, value_rows, grad_out, log_decay):
    n = lax.axis_size("seq")
    dp = lax.axis_size("dp")
    bits = dp.bit_length() - 1
    length, width = queries.shape[1:]
    heads = log_decay.shape[2]
    features = layer_input.shape[2]
    cols = features // n
    size = cols // 2 // CHUNKS
    parts = 2 * GROUPS
    wide = width // GROUPS
    tot_rows = -(-heads // 8) * 8
    factor = 1.0 / math.sqrt(dp * n * length)
    vmem = pl.BlockSpec(memory_space=pltpu.VMEM)
    dma = pltpu.SemaphoreType.DMA
    tile = (heads, DH, DH)
    grads = pl.pallas_call(
        functools.partial(kernel, n, bits, heads, factor),
        out_shape=[jax.ShapeDtypeStruct((length, width), BF16)] * 3
        + [jax.ShapeDtypeStruct((cols, width), BF16)] * 2,
        in_specs=[pl.BlockSpec(memory_space=pltpu.HBM)] * 5 + [vmem],
        out_specs=[vmem] * 5,
        scratch_shapes=[pltpu.VMEM((length, width), BF16)] * 4
        + [
            pltpu.VMEM((heads, length, DH), F32),
            pltpu.VMEM((tot_rows, DH), F32),
            pltpu.VMEM(tile, BF16),
            pltpu.VMEM(tile, BF16),
            pltpu.VMEM((n - 1,) + tile, BF16),
            pltpu.VMEM((n - 1,) + tile, BF16),
            pltpu.VMEM((n - 1, tot_rows, DH), F32),
            pltpu.VMEM((n - 1, tot_rows, DH), F32),
            pltpu.VMEM((tot_rows, DH), F32),
            pltpu.VMEM((tot_rows, DH), F32),
            pltpu.VMEM(tile, F32),
            pltpu.VMEM(tile, F32),
            pltpu.VMEM((length, width), F32),
            pltpu.VMEM((length, width), F32),
            pltpu.VMEM((length, width), F32),
            pltpu.VMEM((n, length, cols), BF16),
            pltpu.VMEM((cols, n * length), BF16),
            pltpu.VMEM((parts, n, length, wide), BF16),
            pltpu.VMEM((parts, CHUNKS, size, wide), BF16),
            pltpu.VMEM((parts, CHUNKS, size, wide), BF16),
            pltpu.VMEM((bits - 1, parts, CHUNKS, size, wide), BF16),
            pltpu.VMEM((bits - 1, parts, CHUNKS, size, wide), BF16),
            dma((4,)), dma((4, n - 1)), dma((4, n - 1)),
            dma((PIECES, n - 1)), dma((PIECES, n - 1)),
            dma((PIECES, n - 1)), dma((PIECES, n - 1)), dma,
            dma((2, parts, n - 1)), dma((2, parts, n - 1)),
            dma((parts, CHUNKS)), dma((parts, CHUNKS)),
            dma((bits - 1, parts, CHUNKS)), dma((bits - 1, parts, CHUNKS)),
            dma((parts, CHUNKS)), dma((parts, CHUNKS)),
        ],
        compiler_params=pltpu.CompilerParams(
            collective_id=0, has_side_effects=True, vmem_limit_bytes=48 << 20
        ),
    )(layer_input[0], queries[0], key_rows[0], value_rows[0], grad_out[0], log_decay[0])
    return (grads[0][None], grads[1][None], grads[2][None], grads[3], grads[4])


def solution(mesh):
    return jax.shard_map(
        per_device,
        mesh=mesh,
        in_specs=(
            P("dp", "seq", None),
            P("dp", "seq", "head"),
            P("dp", "seq", "head"),
            P("dp", "seq", "head"),
            P("dp", "seq", "head"),
            P("dp", "seq", "head"),
        ),
        out_specs=(
            P("dp", "seq", "head"),
            P("dp", "seq", "head"),
            P("dp", "seq", "head"),
            P("seq", "head"),
            P("seq", "head"),
        ),
        check_vma=False,
    )
```

time: 120 us -> 97 us (0.81)
  Pallas kernels: 109 us -> 86.1 us
    pallas_call x1, Pallas kernels: 109 us -> 86.1 us  [per_device(): pl.pallas_call(functools.partial(kernel, n, bits, heads, factor), out_sha...]
where the time goes in v2:
time: 97 us; the launch traced here: 96.8 us
  Pallas kernels  86.1 us (89%)
  local copies, waits for them, and re-layouts  10.1 us (10%)
    pallas_call x1, Pallas kernels, per_device(): pl.pallas_call(functools.partial(kernel, n, bits, heads, factor), out_sha...  86.1 us
    unnamed x16, local copies, waits for them, and re-layouts  10.1 us

profile of v2, /device:TPU:0, one launch (start us, length us, event | category | flops | bytes accessed | tf_op | source)
XLA Modules:
  0.0 96.8 jit_solution(5445963730849350687)
XLA Ops:
  0.6 0.8 copy.11
  1.4 0.0 copy-start
  1.4 1.4 %copy-done = bf16[1,128,6144]{2,1,0:T(8,128)(2,1)S(1)} copy-done((bf16[1,128,6144]{2,1,0:T(8,128)(2,1)S(1)}, bf16[1,128,6144]{2,1,0:T(8,128)(2,1)}, u32[]{:S(2)}) %copy-start) | copy-done | bytes 1572888
  2.8 0.0 copy-start.1
  2.8 0.9 copy-done.1
  3.7 0.0 copy-start.2
  3.7 0.9 copy-done.2
  4.6 0.0 copy-start.3
  4.6 0.9 copy-done.3
  5.5 0.0 copy-start.4
  5.5 0.9 copy-done.4
  6.4 86.1 %shard_map.101 = (bf16[128,512]{1,0:T(8,128)(2,1)S(1)}, bf16[128,512]{1,0:T(8,128)(2,1)S(1)}, bf16[128,512]{1,0:T(8,128)(2,1)S(1)}, bf16[1536,512]{1,0:T(8,128)(2,1)S(1)}, bf16[1536,512]{1,0:T(8,128)(2,1)S(1)}) custom-call(bf16[128,6144]{1,0:T(8,128)(2,1)S(1)} %bitcast.9, bf16[128,512]{1,0:T(8,128)(2,1)S(1)} %bitcast.11, bf16[128,512]{1,0:T(8,128)(2,1)S(1)} %bitcast.12, ...), custom_call_target="tpu_custom_call" | custom-call | tf_op jit(solution)/shard_map/pallas_call | solution.py:380
  92.5 0.7 copy.17
  93.2 0.7 copy.18
  93.9 0.7 copy.19
  94.5 1.1 %copy.20 = bf16[1536,512]{1,0:T(8,128)(2,1)} copy(bf16[1536,512]{1,0:T(8,128)(2,1)S(1)} %get-tuple-element.23) | data formatting | bytes 3145728
  95.7 1.1 %copy.21 = bf16[1536,512]{1,0:T(8,128)(2,1)} copy(bf16[1536,512]{1,0:T(8,128)(2,1)S(1)} %get-tuple-element.24) | data formatting | bytes 3145728
Async XLA Ops:
  1.4 1.4 %copy-start = (bf16[1,128,6144]{2,1,0:T(8,128)(2,1)S(1)}, bf16[1,128,6144]{2,1,0:T(8,128)(2,1)}, u32[]{:S(2)}) copy-start(bf16[1,128,6144]{2,1,0:T(8,128)(2,1)} %param.6) | copy-start | bytes 4718596
  2.8 0.9 copy-start.1
  3.7 0.9 copy-start.2
  4.6 0.9 copy-start.3
  5.5 0.9 copy-start.4

commit v3 on v2

--- a/solution.py
+++ b/solution.py
@@ -9,7 +9,6 @@
 from jax.sharding import PartitionSpec as P
 
 DH = 128
-CHUNKS = 2
 GROUPS = 2
 PIECES = 3
 MESH = pl.DeviceIdType.MESH
@@ -29,25 +28,25 @@
 def kernel(
     n, bits, heads, factor,
     x_hbm, q_hbm, k_hbm, v_hbm, g_hbm, ld_ref,
-    gq_ref, gk_ref, gv_ref, ok_ref, ov_ref,
+    gq_hbm, gk_hbm, gv_hbm, ok_hbm, ov_hbm,
+    gq_ref, gk_ref, gv_ref, done,
     q_ref, k_ref, v_ref, g_ref,
     cum_s, tot_s, kst_own, qst_own, kst, qst, tot_b, tot_a, w_b, w_a, pre, suf,
     acc_q, acc_k, acc_v, rx, rxt, gg, half_send, half_recv, lev_send, lev_recv,
     in_sem, st_send, st_recv, x_send, x_recv, xf_send, xf_recv, x_sem, g_send, g_recv,
-    c_send, c_recv, l_send, l_recv, f_send, f_recv,
+    c_send, c_recv, l_send, l_recv, f_send, f_recv, o_sem, small_sem,
 ):
     s = lax.axis_index("seq")
     d = lax.axis_index("dp")
     head = lax.axis_index("head")
     length = q_ref.shape[0]
     cols = rx.shape[2]
-    half = cols // 2
-    size = half // CHUNKS
     piece = cols // PIECES
+    size = piece // 2
     group = heads // GROUPS
     parts = 2 * GROUPS
     wide = gg.shape[3]
-    outs = (ok_ref, ov_ref)
+    outs = (ok_hbm, ov_hbm)
 
     def partner(bit):
         block = 1 << bit
@@ -166,13 +165,6 @@
         to_end = jnp.exp(cum[length - 1 : length, :] - cum)
         keys = (k_ref[:, at].astype(F32) * to_end).astype(BF16)
         kst_own[h] = dot(keys, v_ref[:, at], TN).astype(BF16)
-    for i in range(1, PIECES):
-        x_start(i)
-    for step in range(n - 1, 0, -1):
-        @pl.when(s + step < n)
-        def _(step=step):
-            for copy in forward(step):
-                copy.start()
 
     for h in range(heads):
         at = pl.ds(h * DH, DH)
@@ -251,9 +243,23 @@
             def _(way=way, part=part):
                 relay(way, part, 0).start()
 
+    for i in range(1, PIECES):
+        x_start(i)
+    for step in range(n - 1, 0, -1):
+        @pl.when(s + step < n)
+        def _(step=step):
+            for copy in forward(step):
+                copy.start()
+    writes = [
+        pltpu.make_async_copy(src, dst, small_sem.at[i])
+        for i, (src, dst) in enumerate(((gk_ref, gk_hbm), (gv_ref, gv_hbm), (gq_ref, gq_hbm)))
+    ]
+    writes[0].start()
+    writes[1].start()
+
     low = lax.rem(d, 2)
-    own_row = low * half
-    far_row = (1 - low) * half
+    own_row = low * size
+    far_row = (1 - low) * size
 
     def product(start, part):
         rows = rxt[pl.ds(pl.multiple_of(start, 16), size), :]
@@ -274,36 +280,33 @@
 
     halves, levels, finals = {}, {}, {}
 
-    def multiply(part):
-        for i in range(CHUNKS):
-            half_send[part, i] = product(far_row + i * size, part).astype(BF16)
-            halves[part, i] = exchange(
-                half_send.at[part, i], half_recv.at[part, i],
-                c_send.at[part, i], c_recv.at[part, i], near,
-            )
-            halves[part, i].start()
-        for i in range(CHUNKS):
-            total = product(own_row + i * size, part)
-            halves[part, i].wait_recv()
-            total = total + half_recv[part, i].astype(F32)
-            lev_send[0, part, i] = total.astype(BF16)
-            level_up(0, part, i)
+    def multiply(i, part):
+        half_send[part, i] = product(far_row + i * piece, part).astype(BF16)
+        halves[part, i] = exchange(
+            half_send.at[part, i], half_recv.at[part, i],
+            c_send.at[part, i], c_recv.at[part, i], near,
+        )
+        halves[part, i].start()
+        total = product(own_row + i * piece, part)
+        halves[part, i].wait_recv()
+        total = total + half_recv[part, i].astype(F32)
+        lev_send[0, part, i] = total.astype(BF16)
+        level_up(0, part, i)
 
     pass_on(0, 0)
-    for i in range(1, PIECES):
-        x_swap(i)
     x_own.wait()
     x_turn(0)
     for wave in range(1, parts + n - 2):
         for part in range(parts):
             if 0 <= wave - part < n - 1:
                 pass_on(part, wave - part)
-        if wave <= n - 2:
-            for i in range(1, PIECES):
-                if (i - 1) * (n - 2) // (PIECES - 1) == wave - 1:
-                    x_turn(i)
         if wave >= n - 2:
-            multiply(wave - (n - 2))
+            multiply(0, wave - (n - 2))
+    for i in range(1, PIECES):
+        x_swap(i)
+        x_turn(i)
+        for part in range(parts):
+            multiply(i, part)
 
     for step in range(1, n):
         @pl.when(s >= step)
@@ -318,10 +321,11 @@
         at = pl.ds(h * DH, DH)
         carried = jnp.exp(cum_s[h]) * dot(g_ref[:, at], pre[h].astype(BF16), NT)
         gq_ref[:, at] = ((acc_q[:, at] + carried) * scale).astype(BF16)
+    writes[2].start()
 
     for level in range(bits - 1):
-        for part in range(parts):
-            for i in range(CHUNKS):
+        for i in range(PIECES):
+            for part in range(parts):
                 levels[level, part, i].wait_recv()
                 total = lev_send[level, part, i].astype(F32) + lev_recv[level, part, i].astype(F32)
                 if level < bits - 2:
@@ -329,12 +333,15 @@
                     level_up(level + 1, part, i)
                     continue
                 here = outs[part // GROUPS].at[
-                    pl.ds(pl.multiple_of(own_row + i * size, 16), size),
+                    pl.ds(pl.multiple_of(own_row + i * piece, 16), size),
                     pl.ds((part % GROUPS) * wide, wide),
                 ]
-                here[...] = (total * factor).astype(BF16)
+                done[part, i] = (total * factor).astype(BF16)
+                copy = pltpu.make_async_copy(done.at[part, i], here, o_sem.at[part, i])
+                copy.start()
+                writes.append(copy)
                 finals[part, i] = exchange(
-                    here, here, f_send.at[part, i], f_recv.at[part, i], near
+                    done.at[part, i], here, f_send.at[part, i], f_recv.at[part, i], near
                 )
                 finals[part, i].start()
 
@@ -357,7 +364,16 @@
     for copies in (x_copies, x_swaps, halves, levels):
         for copy in copies.values():
             copy.wait_send()
-    for copy in finals.values():
+    for copy in list(finals.values()) + writes:
+        copy.wait()
+
+
+def emit(*refs):
+    sems = refs[-1]
+    copies = [pltpu.make_async_copy(refs[i], refs[5 + i], sems.at[i]) for i in range(5)]
+    for copy in copies:
+        copy.start()
+    for copy in copies:
         copy.wait()
 
 
@@ -369,7 +385,7 @@
     heads = log_decay.shape[2]
     features = layer_input.shape[2]
     cols = features // n
-    size = cols // 2 // CHUNKS
+    size = cols // PIECES // 2
     parts = 2 * GROUPS
     wide = width // GROUPS
     tot_rows = -(-heads // 8) * 8
@@ -382,8 +398,10 @@
         out_shape=[jax.ShapeDtypeStruct((length, width), BF16)] * 3
         + [jax.ShapeDtypeStruct((cols, width), BF16)] * 2,
         in_specs=[pl.BlockSpec(memory_space=pltpu.HBM)] * 5 + [vmem],
-        out_specs=[vmem] * 5,
-        scratch_shapes=[pltpu.VMEM((length, width), BF16)] * 4
+        out_specs=[pl.BlockSpec(memory_space=pltpu.HBM)] * 5,
+        scratch_shapes=[pltpu.VMEM((length, width), BF16)] * 3
+        + [pltpu.VMEM((parts, PIECES, size, wide), BF16)]
+        + [pltpu.VMEM((length, width), BF16)] * 4
         + [
             pltpu.VMEM((heads, length, DH), F32),
             pltpu.VMEM((tot_rows, DH), F32),
@@ -403,22 +421,31 @@
             pltpu.VMEM((n, length, cols), BF16),
             pltpu.VMEM((cols, n * length), BF16),
             pltpu.VMEM((parts, n, length, wide), BF16),
-            pltpu.VMEM((parts, CHUNKS, size, wide), BF16),
-            pltpu.VMEM((parts, CHUNKS, size, wide), BF16),
-            pltpu.VMEM((bits - 1, parts, CHUNKS, size, wide), BF16),
-            pltpu.VMEM((bits - 1, parts, CHUNKS, size, wide), BF16),
+            pltpu.VMEM((parts, PIECES, size, wide), BF16),
+            pltpu.VMEM((parts, PIECES, size, wide), BF16),
+            pltpu.VMEM((bits - 1, parts, PIECES, size, wide), BF16),
+            pltpu.VMEM((bits - 1, parts, PIECES, size, wide), BF16),
             dma((4,)), dma((4, n - 1)), dma((4, n - 1)),
             dma((PIECES, n - 1)), dma((PIECES, n - 1)),
             dma((PIECES, n - 1)), dma((PIECES, n - 1)), dma,
             dma((2, parts, n - 1)), dma((2, parts, n - 1)),
-            dma((parts, CHUNKS)), dma((parts, CHUNKS)),
-            dma((bits - 1, parts, CHUNKS)), dma((bits - 1, parts, CHUNKS)),
-            dma((parts, CHUNKS)), dma((parts, CHUNKS)),
+            dma((parts, PIECES)), dma((parts, PIECES)),
+            dma((bits - 1, parts, PIECES)), dma((bits - 1, parts, PIECES)),
+            dma((parts, PIECES)), dma((parts, PIECES)),
+            dma((parts, PIECES)), dma((3,)),
         ],
         compiler_params=pltpu.CompilerParams(
-            collective_id=0, has_side_effects=True, vmem_limit_bytes=48 << 20
+            collective_id=0, has_side_effects=True, vmem_limit_bytes=60 << 20
         ),
     )(layer_input[0], queries[0], key_rows[0], value_rows[0], grad_out[0], log_decay[0])
+    hbm = pl.BlockSpec(memory_space=pltpu.HBM)
+    grads = pl.pallas_call(
+        emit,
+        out_shape=[jax.ShapeDtypeStruct(a.shape, a.dtype) for a in grads],
+        in_specs=[hbm] * 5,
+        out_specs=[hbm] * 5,
+        scratch_shapes=[dma((5,))],
+    )(*grads)
     return (grads[0][None], grads[1][None], grads[2][None], grads[3], grads[4])
 
 

time: 97 us -> 217 us (2.24)
  Pallas kernels: 86.1 us -> 215 us
  local copies, waits for them, and re-layouts: 10.1 us -> 1.42 us
    pallas_call x0 -> x1, Pallas kernels: none -> 108 us  [per_device(): pl.pallas_call(emit, out_shape=[jax.ShapeDtypeStruct(a.shape, a.dtype) fo...]
    pallas_call x1, Pallas kernels: 86.1 us -> 107 us  [per_device(): pl.pallas_call(functools.partial(kernel, n, bits, heads, factor), out_sha...]
    unnamed x16 -> x1, local copies, waits for them, and re-layouts: 10.1 us -> 1.42 us
where the time goes in v3:
time: 217 us
  Pallas kernels  215 us (99%)
    pallas_call x1, Pallas kernels, per_device(): pl.pallas_call(emit, out_shape=[jax.ShapeDtypeStruct(a.shape, a.dtype) fo...  108 us
    pallas_call x1, Pallas kernels, per_device(): pl.pallas_call(functools.partial(kernel, n, bits, heads, factor), out_sha...  107 us

profile of v3, /device:TPU:0, one launch (start us, length us, event | category | flops | bytes accessed | tf_op | source)
XLA Modules:
  0.0 217.3 jit_solution(16747227007357852835)
XLA Ops:
  0.6 1.4 copy.11
  2.0 106.9 %shard_map.101 = (bf16[128,512]{1,0:T(8,128)(2,1)}, bf16[128,512]{1,0:T(8,128)(2,1)}, bf16[128,512]{1,0:T(8,128)(2,1)}, bf16[1536,512]{1,0:T(8,128)(2,1)}, bf16[1536,512]{1,0:T(8,128)(2,1)}) custom-call(bf16[128,6144]{1,0:T(8,128)(2,1)} %bitcast.9, bf16[128,512]{1,0:T(8,128)(2,1)} %bitcast.11, bf16[128,512]{1,0:T(8,128)(2,1)} %bitcast.12, ...), custom_call_target="tpu_custom_call" | custom-call | tf_op jit(solution)/shard_map/pallas_call | solution.py:396
  108.9 108.4 %shard_map.102 = (bf16[128,512]{1,0:T(8,128)(2,1)}, bf16[128,512]{1,0:T(8,128)(2,1)}, bf16[128,512]{1,0:T(8,128)(2,1)}, bf16[1536,512]{1,0:T(8,128)(2,1)}, bf16[1536,512]{1,0:T(8,128)(2,1)}) custom-call(bf16[128,512]{1,0:T(8,128)(2,1)} %get-tuple-element.15.refs_0_, bf16[128,512]{1,0:T(8,128)(2,1)} %get-tuple-element.16.refs_1_, ...), custom_call_target="tpu_custom_call" | custom-call | tf_op jit(solution)/shard_map/pallas_call | solution.py:442

commit v4 on v3

--- a/solution.py
+++ b/solution.py
@@ -28,13 +28,12 @@
 def kernel(
     n, bits, heads, factor,
     x_hbm, q_hbm, k_hbm, v_hbm, g_hbm, ld_ref,
-    gq_hbm, gk_hbm, gv_hbm, ok_hbm, ov_hbm,
-    gq_ref, gk_ref, gv_ref, done,
+    gq_ref, gk_ref, gv_ref, ok_ref, ov_ref,
     q_ref, k_ref, v_ref, g_ref,
     cum_s, tot_s, kst_own, qst_own, kst, qst, tot_b, tot_a, w_b, w_a, pre, suf,
     acc_q, acc_k, acc_v, rx, rxt, gg, half_send, half_recv, lev_send, lev_recv,
     in_sem, st_send, st_recv, x_send, x_recv, xf_send, xf_recv, x_sem, g_send, g_recv,
-    c_send, c_recv, l_send, l_recv, f_send, f_recv, o_sem, small_sem,
+    c_send, c_recv, l_send, l_recv, f_send, f_recv,
 ):
     s = lax.axis_index("seq")
     d = lax.axis_index("dp")
@@ -46,7 +45,7 @@
     group = heads // GROUPS
     parts = 2 * GROUPS
     wide = gg.shape[3]
-    outs = (ok_hbm, ov_hbm)
+    outs = (ok_ref, ov_ref)
 
     def partner(bit):
         block = 1 << bit
@@ -250,12 +249,6 @@
         def _(step=step):
             for copy in forward(step):
                 copy.start()
-    writes = [
-        pltpu.make_async_copy(src, dst, small_sem.at[i])
-        for i, (src, dst) in enumerate(((gk_ref, gk_hbm), (gv_ref, gv_hbm), (gq_ref, gq_hbm)))
-    ]
-    writes[0].start()
-    writes[1].start()
 
     low = lax.rem(d, 2)
     own_row = low * size
@@ -321,7 +314,6 @@
         at = pl.ds(h * DH, DH)
         carried = jnp.exp(cum_s[h]) * dot(g_ref[:, at], pre[h].astype(BF16), NT)
         gq_ref[:, at] = ((acc_q[:, at] + carried) * scale).astype(BF16)
-    writes[2].start()
 
     for level in range(bits - 1):
         for i in range(PIECES):
@@ -336,12 +328,9 @@
                     pl.ds(pl.multiple_of(own_row + i * piece, 16), size),
                     pl.ds((part % GROUPS) * wide, wide),
                 ]
-                done[part, i] = (total * factor).astype(BF16)
-                copy = pltpu.make_async_copy(done.at[part, i], here, o_sem.at[part, i])
-                copy.start()
-                writes.append(copy)
+                here[...] = (total * factor).astype(BF16)
                 finals[part, i] = exchange(
-                    done.at[part, i], here, f_send.at[part, i], f_recv.at[part, i], near
+                    here, here, f_send.at[part, i], f_recv.at[part, i], near
                 )
                 finals[part, i].start()
 
@@ -364,16 +353,7 @@
     for copies in (x_copies, x_swaps, halves, levels):
         for copy in copies.values():
             copy.wait_send()
-    for copy in list(finals.values()) + writes:
-        copy.wait()
-
-
-def emit(*refs):
-    sems = refs[-1]
-    copies = [pltpu.make_async_copy(refs[i], refs[5 + i], sems.at[i]) for i in range(5)]
-    for copy in copies:
-        copy.start()
-    for copy in copies:
+    for copy in finals.values():
         copy.wait()
 
 
@@ -398,10 +378,8 @@
         out_shape=[jax.ShapeDtypeStruct((length, width), BF16)] * 3
         + [jax.ShapeDtypeStruct((cols, width), BF16)] * 2,
         in_specs=[pl.BlockSpec(memory_space=pltpu.HBM)] * 5 + [vmem],
-        out_specs=[pl.BlockSpec(memory_space=pltpu.HBM)] * 5,
-        scratch_shapes=[pltpu.VMEM((length, width), BF16)] * 3
-        + [pltpu.VMEM((parts, PIECES, size, wide), BF16)]
-        + [pltpu.VMEM((length, width), BF16)] * 4
+        out_specs=[vmem] * 5,
+        scratch_shapes=[pltpu.VMEM((length, width), BF16)] * 4
         + [
             pltpu.VMEM((heads, length, DH), F32),
             pltpu.VMEM((tot_rows, DH), F32),
@@ -432,20 +410,11 @@
             dma((parts, PIECES)), dma((parts, PIECES)),
             dma((bits - 1, parts, PIECES)), dma((bits - 1, parts, PIECES)),
             dma((parts, PIECES)), dma((parts, PIECES)),
-            dma((parts, PIECES)), dma((3,)),
         ],
         compiler_params=pltpu.CompilerParams(
-            collective_id=0, has_side_effects=True, vmem_limit_bytes=60 << 20
+            collective_id=0, has_side_effects=True, vmem_limit_bytes=48 << 20
         ),
     )(layer_input[0], queries[0], key_rows[0], value_rows[0], grad_out[0], log_decay[0])
-    hbm = pl.BlockSpec(memory_space=pltpu.HBM)
-    grads = pl.pallas_call(
-        emit,
-        out_shape=[jax.ShapeDtypeStruct(a.shape, a.dtype) for a in grads],
-        in_specs=[hbm] * 5,
-        out_specs=[hbm] * 5,
-        scratch_shapes=[dma((5,))],
-    )(*grads)
     return (grads[0][None], grads[1][None], grads[2][None], grads[3], grads[4])
 
 

time: 217 us -> 117 us (0.54)
  Pallas kernels: 215 us -> 106 us
  local copies, waits for them, and re-layouts: 1.42 us -> 10.1 us
    pallas_call x1 -> x0, Pallas kernels: 108 us -> none  [per_device(): pl.pallas_call(emit, out_shape=[jax.ShapeDtypeStruct(a.shape, a.dtype) fo...]
    unnamed x1 -> x16, local copies, waits for them, and re-layouts: 1.42 us -> 10.1 us
where the time goes in v4:
time: 117 us
  Pallas kernels  106 us (91%)
  local copies, waits for them, and re-layouts  10.1 us (9%)
    pallas_call x1, Pallas kernels, per_device(): pl.pallas_call(functools.partial(kernel, n, bits, heads, factor), out_sha...  106 us
    unnamed x16, local copies, waits for them, and re-layouts  10.1 us

profile of v4, /device:TPU:0, one launch (start us, length us, event | category | flops | bytes accessed | tf_op | source)
XLA Modules:
  0.0 116.9 jit_solution(6692807923040406179)
XLA Ops:
  0.6 0.8 copy.11
  1.4 0.0 copy-start
  1.4 1.4 %copy-done = bf16[1,128,6144]{2,1,0:T(8,128)(2,1)S(1)} copy-done((bf16[1,128,6144]{2,1,0:T(8,128)(2,1)S(1)}, bf16[1,128,6144]{2,1,0:T(8,128)(2,1)}, u32[]{:S(2)}) %copy-start) | copy-done | bytes 1572888
  2.8 0.0 copy-start.1
  2.8 0.9 copy-done.1
  3.7 0.0 copy-start.2
  3.7 0.9 copy-done.2
  4.6 0.0 copy-start.3
  4.6 0.9 copy-done.3
  5.5 0.0 copy-start.4
  5.5 0.9 copy-done.4
  6.4 106.2 %shard_map.101 = (bf16[128,512]{1,0:T(8,128)(2,1)S(1)}, bf16[128,512]{1,0:T(8,128)(2,1)S(1)}, bf16[128,512]{1,0:T(8,128)(2,1)S(1)}, bf16[1536,512]{1,0:T(8,128)(2,1)S(1)}, bf16[1536,512]{1,0:T(8,128)(2,1)S(1)}) custom-call(bf16[128,6144]{1,0:T(8,128)(2,1)S(1)} %bitcast.9, bf16[128,512]{1,0:T(8,128)(2,1)S(1)} %bitcast.11, bf16[128,512]{1,0:T(8,128)(2,1)S(1)} %bitcast.12, ...), custom_call_target="tpu_custom_call" | custom-call | tf_op jit(solution)/shard_map/pallas_call | solution.py:376
  112.6 0.7 copy.17
  113.3 0.7 copy.18
  113.9 0.7 copy.19
  114.6 1.1 copy.20
  115.7 1.1 copy.21
Async XLA Ops:
  1.4 1.4 %copy-start = (bf16[1,128,6144]{2,1,0:T(8,128)(2,1)S(1)}, bf16[1,128,6144]{2,1,0:T(8,128)(2,1)}, u32[]{:S(2)}) copy-start(bf16[1,128,6144]{2,1,0:T(8,128)(2,1)} %param.6) | copy-start | bytes 4718596
  2.8 0.9 copy-start.1
  3.7 0.9 copy-start.2
  4.6 0.9 copy-start.3
  5.5 0.9 copy-start.4

commit v5 on v4

--- a/solution.py
+++ b/solution.py
@@ -165,6 +165,14 @@
         keys = (k_ref[:, at].astype(F32) * to_end).astype(BF16)
         kst_own[h] = dot(keys, v_ref[:, at], TN).astype(BF16)
 
+    for i in range(1, PIECES):
+        x_start(i)
+    for step in range(n - 1, 0, -1):
+        @pl.when(s + step < n)
+        def _(step=step):
+            for copy in forward(step):
+                copy.start()
+
     for h in range(heads):
         at = pl.ds(h * DH, DH)
         cum = cum_s[h]
@@ -242,13 +250,6 @@
             def _(way=way, part=part):
                 relay(way, part, 0).start()
 
-    for i in range(1, PIECES):
-        x_start(i)
-    for step in range(n - 1, 0, -1):
-        @pl.when(s + step < n)
-        def _(step=step):
-            for copy in forward(step):
-                copy.start()
 
     low = lax.rem(d, 2)
     own_row = low * size
@@ -293,10 +294,12 @@
         for part in range(parts):
             if 0 <= wave - part < n - 1:
                 pass_on(part, wave - part)
+        if wave == n - 2:
+            for i in range(1, PIECES):
+                x_swap(i)
         if wave >= n - 2:
             multiply(0, wave - (n - 2))
     for i in range(1, PIECES):
-        x_swap(i)
         x_turn(i)
         for part in range(parts):
             multiply(i, part)

time: 117 us -> 98.4 us (0.84)
  Pallas kernels: 106 us -> 87.4 us
    pallas_call x1, Pallas kernels: 106 us -> 87.4 us  [per_device(): pl.pallas_call(functools.partial(kernel, n, bits, heads, factor), out_sha...]
where the time goes in v5:
time: 98.4 us; the launch traced here: 98.1 us
  Pallas kernels  87.4 us (89%)
  local copies, waits for them, and re-layouts  10.1 us (10%)
    pallas_call x1, Pallas kernels, per_device(): pl.pallas_call(functools.partial(kernel, n, bits, heads, factor), out_sha...  87.4 us
    unnamed x16, local copies, waits for them, and re-layouts  10.1 us

profile of v5, /device:TPU:0, one launch (start us, length us, event | category | flops | bytes accessed | tf_op | source)
XLA Modules:
  0.0 98.1 jit_solution(11806840081783012242)
XLA Ops:
  0.6 0.8 copy.11
  1.4 0.0 copy-start
  1.4 1.4 %copy-done = bf16[1,128,6144]{2,1,0:T(8,128)(2,1)S(1)} copy-done((bf16[1,128,6144]{2,1,0:T(8,128)(2,1)S(1)}, bf16[1,128,6144]{2,1,0:T(8,128)(2,1)}, u32[]{:S(2)}) %copy-start) | copy-done | bytes 1572888
  2.8 0.0 copy-start.1
  2.8 0.9 copy-done.1
  3.7 0.0 copy-start.2
  3.7 0.9 copy-done.2
  4.6 0.0 copy-start.3
  4.6 0.9 copy-done.3
  5.5 0.0 copy-start.4
  5.5 0.9 copy-done.4
  6.4 87.4 %shard_map.101 = (bf16[128,512]{1,0:T(8,128)(2,1)S(1)}, bf16[128,512]{1,0:T(8,128)(2,1)S(1)}, bf16[128,512]{1,0:T(8,128)(2,1)S(1)}, bf16[1536,512]{1,0:T(8,128)(2,1)S(1)}, bf16[1536,512]{1,0:T(8,128)(2,1)S(1)}) custom-call(bf16[128,6144]{1,0:T(8,128)(2,1)S(1)} %bitcast.9, bf16[128,512]{1,0:T(8,128)(2,1)S(1)} %bitcast.11, bf16[128,512]{1,0:T(8,128)(2,1)S(1)} %bitcast.12, ...), custom_call_target="tpu_custom_call" | custom-call | tf_op jit(solution)/shard_map/pallas_call | solution.py:379
  93.9 0.7 copy.17
  94.5 0.7 copy.18
  95.2 0.7 copy.19
  95.9 1.1 %copy.20 = bf16[1536,512]{1,0:T(8,128)(2,1)} copy(bf16[1536,512]{1,0:T(8,128)(2,1)S(1)} %get-tuple-element.23) | data formatting | bytes 3145728
  97.0 1.1 %copy.21 = bf16[1536,512]{1,0:T(8,128)(2,1)} copy(bf16[1536,512]{1,0:T(8,128)(2,1)S(1)} %get-tuple-element.24) | data formatting | bytes 3145728
Async XLA Ops:
  1.4 1.4 %copy-start = (bf16[1,128,6144]{2,1,0:T(8,128)(2,1)S(1)}, bf16[1,128,6144]{2,1,0:T(8,128)(2,1)}, u32[]{:S(2)}) copy-start(bf16[1,128,6144]{2,1,0:T(8,128)(2,1)} %param.6) | copy-start | bytes 4718596
  2.8 0.9 copy-start.1
  3.7 0.9 copy-start.2
  4.6 0.9 copy-start.3
  5.5 0.9 copy-start.4
